TPU v7x, 256 devices: a whole 4x4x8 slice. The times are simulated.
256 devices in a mesh: sample: 16 (over z, x_hi), seq: 16 (over y, x_lo, core).
Axes of the slice: x: 4 (x_hi: 2, x_lo: 2; x = x_hi * 2 + x_lo), y: 4, z: 8, core: 2. Of those that a mesh axis runs over, the one named last changes fastest.
Arguments:
- queries: bfloat16 [16, 2048, 8192], P('sample', 'seq'), may hold values from -900 to 900
- span_keys: bfloat16 [16, 2048, 1024], P('sample', 'seq'), may hold values from -6 to 6
- span_values: bfloat16 [16, 2048, 1024], P('sample', 'seq'), may hold values from -6 to 6
- prompt_keys: bfloat16 [2048, 1024], P('sample'), may hold values from -6 to 6
- prompt_values: bfloat16 [2048, 1024], P('sample'), may hold values from -6 to 6
- lengths: int32 [16], P('sample'), may hold values from 512 to 8192, as said below
- offsets: int32 [16], P('sample'), may hold values from 0 to 6144, as said below
Outputs:
- attended: bfloat16 [16, 2048, 8192], P('sample', 'seq')
Inputs may be any that keep to these rules, and one draw needn't show every extreme that they name: A completion's block holds at least 512 live tokens: lengths[c] - offsets[c] >= 512. `offsets`: each offset is a whole multiple of 2048.
All inputs are finite; a program needn't handle non-finite values.
Results may differ from a plain program's by a relative error of at most 0.012.
The roundings to bfloat16 on the way count: a program that leaves them out, or rounds other values in their place, can miss the bound.
Values may be sent and summed in bfloat16 or wider, within the bound.
No kernel may reach another device: no remote copies, remote signals or barrier semaphores. Data moves between devices by JAX's collectives and lax.ppermute only.
A program may use at most 128 MiB of HBM per device.

v0:
```python
import math
import jax
import jax.numpy as jnp
from jax import lax
from jax.sharding import PartitionSpec as P

HEADS = 64
KV_HEADS = 8
HEAD_DIM = 128
ROPE_BASE = 500000.0
NEG_FILL = -1e30


def rope_angles(positions, head_size):
    half_dim = head_size // 2
    frequency = ROPE_BASE ** (-(jnp.arange(half_dim, dtype=jnp.float32) * (2.0 / head_size)))
    angles = positions.astype(jnp.float32)[:, None] * frequency[None, :]
    return (jnp.cos(angles), jnp.sin(angles))


def rotate(stacked, cos_table, sine_table):
    half_dim = stacked.shape[-1] // 2
    former = stacked[..., :half_dim]
    latter = stacked[..., half_dim:]
    cos_part = cos_table[:, None, :]
    sine_part = sine_table[:, None, :]
    return jnp.concatenate(
        [former * cos_part - latter * sine_part, latter * cos_part + former * sine_part], axis=-1
    )


def absorb(carry_state, query_group, key_rows, value_rows, allowed):
    run_max, run_sum, run_acc = carry_state
    scaling = 1.0 / math.sqrt(query_group.shape[-1])
    scores = (
        jnp.einsum("agqd,kad->agqk", query_group, key_rows, preferred_element_type=jnp.float32)
        * scaling
    )
    if allowed is not None:
        scores = jnp.where(allowed, scores, NEG_FILL)
    new_max = jnp.maximum(run_max, jnp.max(scores, axis=-1))
    weights = jnp.exp(scores - new_max[..., None])
    if allowed is not None:
        weights = jnp.where(allowed, weights, 0.0)
    fade_factor = jnp.exp(run_max - new_max)
    new_sum = run_sum * fade_factor + jnp.sum(weights, axis=-1)
    product = jnp.einsum(
        "agqk,kad->agqd",
        weights.astype(jnp.bfloat16),
        value_rows,
        preferred_element_type=jnp.float32,
    )
    return (new_max, new_sum, run_acc * fade_factor[..., None] + product)


def shards(queries, span_keys, span_values, prompt_keys, prompt_values, lengths, offsets):
    seq_count = lax.axis_size("seq")
    seq_index = lax.axis_index("seq")
    local_rows = queries.shape[1]
    span_len = local_rows * seq_count
    prompt_local = prompt_keys.shape[0]
    prompt_len = prompt_local * lax.axis_size("sample")
    group_size = HEADS // KV_HEADS
    length = lengths[0]
    offset = offsets[0]
    live_count = jnp.clip(length - offset, 0, span_len)
    row_ids = seq_index * local_rows + jnp.arange(local_rows, dtype=jnp.int32)
    cos_table, sine_table = rope_angles(prompt_len + offset + row_ids, HEAD_DIM)
    rotated_q = rotate(
        queries[0].astype(jnp.float32).reshape(local_rows, HEADS, HEAD_DIM), cos_table, sine_table
    ).astype(jnp.bfloat16)
    rotated_k = rotate(
        span_keys[0].astype(jnp.float32).reshape(local_rows, KV_HEADS, HEAD_DIM),
        cos_table,
        sine_table,
    ).astype(jnp.bfloat16)
    grouped = rotated_q.reshape(local_rows, KV_HEADS, 1, group_size, HEAD_DIM).transpose(
        1, 2, 3, 0, 4
    )
    initial = (
        jnp.full((KV_HEADS, 1, group_size, local_rows), NEG_FILL, jnp.float32),
        jnp.zeros((KV_HEADS, 1, group_size, local_rows), jnp.float32),
        jnp.zeros((KV_HEADS, 1, group_size, local_rows, HEAD_DIM), jnp.float32),
    )

    def by_head(carry_state, key_piece, value_piece, allowed):
        key_heads = key_piece.reshape(-1, KV_HEADS, 1, HEAD_DIM).transpose(1, 0, 2, 3)
        value_split = value_piece.reshape(-1, KV_HEADS, 1, HEAD_DIM).transpose(1, 0, 2, 3)

        def one_head(packed):
            query_head, run_max, run_sum, run_acc, key_head, value_head = packed
            return absorb((run_max, run_sum, run_acc), query_head, key_head, value_head, allowed)

        return lax.map(one_head, (grouped,) + tuple(carry_state) + (key_heads, value_split))

    shard_piece = (
        lax.all_gather(prompt_keys, "sample", axis=0, tiled=True),
        lax.all_gather(prompt_values, "sample", axis=0, tiled=True),
    )
    after_prompt = by_head(initial, shard_piece[0], shard_piece[1], None)
    last_row = seq_index * local_rows + local_rows - 1
    any_live = seq_index * local_rows < live_count
    flat_keys = rotated_k.reshape(local_rows, KV_HEADS * HEAD_DIM)
    shard_piece = (
        lax.all_gather(flat_keys, "seq", axis=0, tiled=True),
        lax.all_gather(span_values[0], "seq", axis=0, tiled=True),
    )
    piece_count = shard_piece[0].shape[0]
    key_ids = jnp.arange(piece_count, dtype=jnp.int32)
    allowed = (key_ids[None, :] <= row_ids[:, None]) & (key_ids < live_count)[None, :]
    needed = (jnp.int32(0) <= last_row) & any_live
    final_max, final_sum, final_acc = lax.cond(
        needed,
        lambda: tuple(by_head(after_prompt, shard_piece[0], shard_piece[1], allowed)),
        lambda: tuple(after_prompt),
    )
    safe_sum = jnp.where(final_sum > 0.0, final_sum, 1.0)
    outcome = (
        (final_acc / safe_sum[..., None])
        .transpose(3, 0, 1, 2, 4)
        .reshape(local_rows, HEADS * HEAD_DIM)
    )
    live_mask = row_ids < live_count
    outcome = jnp.where(live_mask[:, None], outcome, 0.0).astype(jnp.bfloat16)
    return outcome.reshape(1, local_rows, HEADS * HEAD_DIM)


def solution(mesh):
    in_specs = (
        P("sample", "seq", None),
        P("sample", "seq", None),
        P("sample", "seq", None),
        P("sample", None),
        P("sample", None),
        P("sample"),
        P("sample"),
    )
    out_specs = P("sample", "seq", None)
    return jax.shard_map(shards, mesh=mesh, in_specs=in_specs, out_specs=out_specs, check_vma=False)
```

profile of v0, /device:TPU:1, one launch (start us, length us, event | category | flops | bytes accessed | tf_op | source)
XLA Modules:
  0.0 418.2 jit_solution(11268256134059771003)
XLA Ops:
  6.5 1.9 copy.31
  8.6 1.8 copy.32
  16.2 1.7 fusion.60
  17.9 4.9 %subtract_convert_fusion = (bf16[128,64,64]{2,0,1:T(8,128)(2,1)S(1)}, bf16[128,64,64]{2,0,1:T(8,128)(2,1)S(1)}) fusion(f32[128,64,64]{2,1,0:T(8,128)S(1)} %get-tuple-element.232, f32[128,64,64]{2,1,0:T(8,128)S(1)} %get-tuple-element.231, f32[128,64]{1,0:T(8,128)S(1)} %copy.30, f32[128,64]{1,0:T(8,128)S(1)} %copy.28), kind=kLoop, calls=%fused_computation.64 | loop fusion | flops 4194304 | bytes 6356992 | tf_op jit(solution)/shard_map/convert.7
  22.8 1.2 maximum_bitcast_fusion
  24.0 91.1 %all-gather.6.cloned.1.call-done = bf16[2048,1024]{0,1:T(8,128)(2,1)} async-done(((bf16[128,1024]{0,1:T(8,128)(2,1)}), bf16[2048,1024]{0,1:T(8,128)(2,1)}) %all-gather.6.cloned.1.call-update) | async-done | bytes 4194320 | tf_op jit(solution)/shard_map/all_gather | solution.py:97
  115.1 104.2 %all-gather.8.cloned.1.call-done = bf16[2048,1024]{0,1:T(8,128)(2,1)} async-done(((bf16[128,1024]{0,1:T(8,128)(2,1)}), bf16[2048,1024]{0,1:T(8,128)(2,1)}) %all-gather.8.cloned.1.call-update) | async-done | bytes 4194320 | tf_op jit(solution)/shard_map/all_gather | solution.py:98
  219.3 62.2 %while.26 = (s32[]{:T(128)}, f32[8,1,8,128]{3,2,1,0:T(8,128)S(1)}, f32[8,1,8,128]{3,2,1,0:T(8,128)S(1)}, f32[8,1,8,128,128]{4,3,2,1,0:T(8,128)}, bf16[8,1,8,128,...) while((s32[]{:T(128)}, f32[8,1,8,128]{3,2,1,0:T(8,128)S(1)}, ...), condition=%wide.region_3.4_spmd, body=%wide.region_0.3_spmd.sunk | while | flops 1090655232 | bytes 27052128 | solution.py:94
  219.3 2.4 multiply_reduce_fusion.2
  221.7 1.6 fusion.75
  223.4 3.7 fusion.77
  227.1 2.4 multiply_reduce_fusion.2
  229.4 1.6 fusion.75
  231.1 3.7 fusion.77
  234.8 2.4 multiply_reduce_fusion.2
  237.2 1.6 fusion.75
  238.9 3.7 fusion.77
  242.6 2.4 multiply_reduce_fusion.2
  245.0 1.6 fusion.75
  246.6 3.7 fusion.77
  250.4 2.4 multiply_reduce_fusion.2
  252.8 1.6 fusion.75
  254.5 3.7 fusion.77
  258.2 2.4 multiply_reduce_fusion.2
  260.6 1.6 fusion.75
  262.2 3.7 fusion.77
  266.0 2.4 multiply_reduce_fusion.2
  268.3 1.6 fusion.75
  270.0 3.7 fusion.77
  273.7 2.4 multiply_reduce_fusion.2
  276.1 1.6 fusion.75
  277.8 3.7 fusion.77
  281.5 38.5 %all-gather.12.cloned.1.call-done = bf16[1,2048,1024]{1,2,0:T(8,128)(2,1)} async-done(((bf16[1,128,1024]{1,2,0:T(8,128)(2,1)}), bf16[1,2048,1024]{1,2,0:T(8,128)(2,1)}) %all-gather.12.cloned.1.call-update) | async-done | bytes 4194320 | tf_op jit(solution)/shard_map/all_gather | solution.py:106
  320.1 81.3 %conditional.1 = ((f32[8,1,8,128]{3,2,1,0:T(8,128)S(1)}, f32[8,1,8,128,128]{4,3,2,1,0:T(8,128)})) conditional(s32[]{:T(128)} %convert_element_type.55, (f32[8,1,8,128]{3,2,1,0:T(8,128)S(1)}, f32[8,1,8,128,128]{4,3,2,1,0:T(8,128)}) %tuple.21, (bf16[2048,1024]{0,1:T(8,128)(2,1)}, bf16[2048,1024]{0,1:T(8,128)(2,1)}, s32[]{:T(128)}, ...), branch_computations={%region_4.5_spmd, %region_5.10_spmd} | conditional | flops 1101797504 | bytes 38149884 | solution.py:112
  320.4 76.4 %while.25 = (s32[]{:T(128)}, f32[8,1,8,128]{3,2,1,0:T(8,128)S(1)}, f32[8,1,8,128,128]{4,3,2,1,0:T(8,128)}, f32[8,1,8,128]{3,2,1,0:T(8,128)S(1)}, f32[8,1,8,128]{...) while((s32[]{:T(128)}, f32[8,1,8,128]{3,2,1,0:T(8,128)S(1)}, ...), condition=%wide.region_9.9_spmd, body=%wide.region_6.8_spmd.sunk | while | flops 1101271040 | bytes 28371068 | solution.py:94
  320.5 2.7 fusion.80
  323.2 2.5 fusion.82
  325.7 4.3 %fusion.84 = f32[8,1,8,128,128]{4,3,2,1,0:T(8,128)} fusion(f32[8,1,8,128,128]{4,3,2,1,0:T(8,128)} %get-tuple-element.374, s32[]{:T(128)S(6)} %copy.59, f32[8,128,2048]{2,1,0:T(8,128)S(1)} %get-tuple-element.357, f32[8,128]{1,0:T(8,128)S(1)} %get-tuple-element.359, pred[128,2048]{1,0:T(8,128)(4,1)S(1)} %get-tuple-element.388, ...), kind=kOutput, calls=%fused_computation.35.clone.1 | convolution fusion | flops 547618816 | bytes 10232832 | tf_op jit(solution)/shard_map/cond/branch_1_fun/while/body/eval_jaxpr/agqk,kad->agqd/dot_general | solution.py:47
  330.0 2.7 fusion.80
  332.7 2.5 fusion.82
  335.2 4.3 %fusion.84 = f32[8,1,8,128,128]{4,3,2,1,0:T(8,128)} fusion(f32[8,1,8,128,128]{4,3,2,1,0:T(8,128)} %get-tuple-element.374, s32[]{:T(128)S(6)} %copy.59, f32[8,128,2048]{2,1,0:T(8,128)S(1)} %get-tuple-element.357, f32[8,128]{1,0:T(8,128)S(1)} %get-tuple-element.359, pred[128,2048]{1,0:T(8,128)(4,1)S(1)} %get-tuple-element.388, ...), kind=kOutput, calls=%fused_computation.35.clone.1 | convolution fusion | flops 547618816 | bytes 10232832 | tf_op jit(solution)/shard_map/cond/branch_1_fun/while/body/eval_jaxpr/agqk,kad->agqd/dot_general | solution.py:47
  339.6 2.7 fusion.80
  342.3 2.5 fusion.82
  344.8 4.3 %fusion.84 = f32[8,1,8,128,128]{4,3,2,1,0:T(8,128)} fusion(f32[8,1,8,128,128]{4,3,2,1,0:T(8,128)} %get-tuple-element.374, s32[]{:T(128)S(6)} %copy.59, f32[8,128,2048]{2,1,0:T(8,128)S(1)} %get-tuple-element.357, f32[8,128]{1,0:T(8,128)S(1)} %get-tuple-element.359, pred[128,2048]{1,0:T(8,128)(4,1)S(1)} %get-tuple-element.388, ...), kind=kOutput, calls=%fused_computation.35.clone.1 | convolution fusion | flops 547618816 | bytes 10232832 | tf_op jit(solution)/shard_map/cond/branch_1_fun/while/body/eval_jaxpr/agqk,kad->agqd/dot_general | solution.py:47
  349.1 2.7 fusion.80
  351.8 2.5 fusion.82
  354.3 4.3 %fusion.84 = f32[8,1,8,128,128]{4,3,2,1,0:T(8,128)} fusion(f32[8,1,8,128,128]{4,3,2,1,0:T(8,128)} %get-tuple-element.374, s32[]{:T(128)S(6)} %copy.59, f32[8,128,2048]{2,1,0:T(8,128)S(1)} %get-tuple-element.357, f32[8,128]{1,0:T(8,128)S(1)} %get-tuple-element.359, pred[128,2048]{1,0:T(8,128)(4,1)S(1)} %get-tuple-element.388, ...), kind=kOutput, calls=%fused_computation.35.clone.1 | convolution fusion | flops 547618816 | bytes 10232832 | tf_op jit(solution)/shard_map/cond/branch_1_fun/while/body/eval_jaxpr/agqk,kad->agqd/dot_general | solution.py:47
  358.6 2.7 fusion.80
  361.3 2.5 fusion.82
  363.9 4.3 %fusion.84 = f32[8,1,8,128,128]{4,3,2,1,0:T(8,128)} fusion(f32[8,1,8,128,128]{4,3,2,1,0:T(8,128)} %get-tuple-element.374, s32[]{:T(128)S(6)} %copy.59, f32[8,128,2048]{2,1,0:T(8,128)S(1)} %get-tuple-element.357, f32[8,128]{1,0:T(8,128)S(1)} %get-tuple-element.359, pred[128,2048]{1,0:T(8,128)(4,1)S(1)} %get-tuple-element.388, ...), kind=kOutput, calls=%fused_computation.35.clone.1 | convolution fusion | flops 547618816 | bytes 10232832 | tf_op jit(solution)/shard_map/cond/branch_1_fun/while/body/eval_jaxpr/agqk,kad->agqd/dot_general | solution.py:47
  368.2 2.7 fusion.80
  370.9 2.5 fusion.82
  373.4 4.3 %fusion.84 = f32[8,1,8,128,128]{4,3,2,1,0:T(8,128)} fusion(f32[8,1,8,128,128]{4,3,2,1,0:T(8,128)} %get-tuple-element.374, s32[]{:T(128)S(6)} %copy.59, f32[8,128,2048]{2,1,0:T(8,128)S(1)} %get-tuple-element.357, f32[8,128]{1,0:T(8,128)S(1)} %get-tuple-element.359, pred[128,2048]{1,0:T(8,128)(4,1)S(1)} %get-tuple-element.388, ...), kind=kOutput, calls=%fused_computation.35.clone.1 | convolution fusion | flops 547618816 | bytes 10232832 | tf_op jit(solution)/shard_map/cond/branch_1_fun/while/body/eval_jaxpr/agqk,kad->agqd/dot_general | solution.py:47
  377.7 2.7 fusion.80
  380.4 2.5 fusion.82
  383.0 4.3 %fusion.84 = f32[8,1,8,128,128]{4,3,2,1,0:T(8,128)} fusion(f32[8,1,8,128,128]{4,3,2,1,0:T(8,128)} %get-tuple-element.374, s32[]{:T(128)S(6)} %copy.59, f32[8,128,2048]{2,1,0:T(8,128)S(1)} %get-tuple-element.357, f32[8,128]{1,0:T(8,128)S(1)} %get-tuple-element.359, pred[128,2048]{1,0:T(8,128)(4,1)S(1)} %get-tuple-element.388, ...), kind=kOutput, calls=%fused_computation.35.clone.1 | convolution fusion | flops 547618816 | bytes 10232832 | tf_op jit(solution)/shard_map/cond/branch_1_fun/while/body/eval_jaxpr/agqk,kad->agqd/dot_general | solution.py:47
  387.3 2.7 fusion.80
  390.0 2.5 fusion.82
  392.5 4.3 %fusion.84 = f32[8,1,8,128,128]{4,3,2,1,0:T(8,128)} fusion(f32[8,1,8,128,128]{4,3,2,1,0:T(8,128)} %get-tuple-element.374, s32[]{:T(128)S(6)} %copy.59, f32[8,128,2048]{2,1,0:T(8,128)S(1)} %get-tuple-element.357, f32[8,128]{1,0:T(8,128)S(1)} %get-tuple-element.359, pred[128,2048]{1,0:T(8,128)(4,1)S(1)} %get-tuple-element.388, ...), kind=kOutput, calls=%fused_computation.35.clone.1 | convolution fusion | flops 547618816 | bytes 10232832 | tf_op jit(solution)/shard_map/cond/branch_1_fun/while/body/eval_jaxpr/agqk,kad->agqd/dot_general | solution.py:47
  396.8 4.6 %copy.80 = f32[8,1,8,128,128]{4,3,2,1,0:T(8,128)} copy(f32[8,1,8,128,128]{4,3,2,1,0:T(8,128)} %get-tuple-element.421) | data formatting | bytes 8388608 | tf_op jit(solution)/shard_map/cond
  401.5 2.9 divide_bitcast_fusion
  404.3 2.7 copy.38
  407.0 2.8 reshape.318
  409.8 1.8 select_convert_fusion
  (70 shorter events, 5.3 us)
Async XLA Ops:
  6.5 6.8 %copy-start.1 = (bf16[1,128,1024]{2,1,0:T(8,128)(2,1)S(1)}, bf16[1,128,1024]{2,1,0:T(8,128)(2,1)}, u32[]{:S(2)}) copy-start(bf16[1,128,1024]{2,1,0:T(8,128)(2,1)} %param.15) | copy-start | bytes 786436
  6.5 8.5 %copy-start = (bf16[1,128,8192]{2,1,0:T(8,128)(2,1)S(1)}, bf16[1,128,8192]{2,1,0:T(8,128)(2,1)}, u32[]{:S(2)}) copy-start(bf16[1,128,8192]{2,1,0:T(8,128)(2,1)} %param.13) | copy-start | bytes 6291460
  6.5 108.5 %all-gather.6.cloned.1.call-start = ((), (), s32[]{:S(2)}) async-start(), calls=%async_computation | async-start | bytes 4456448 | tf_op jit(solution)/shard_map/all_gather | solution.py:97
  8.5 210.8 %all-gather.8.cloned.1.call-start = ((), (), s32[]{:S(2)}) async-start(), calls=%async_computation.1 | async-start | bytes 4456448 | tf_op jit(solution)/shard_map/all_gather | solution.py:98
  10.4 271.1 %all-gather.10.cloned.1.call-start = ((), (), s32[]{:S(2)}) async-start(), calls=%async_computation.2 | async-start | bytes 4456448 | tf_op jit(solution)/shard_map/all_gather | solution.py:105
  13.2 306.8 %all-gather.12.cloned.1.call-start = ((), (), s32[]{:S(2)}) async-start(), calls=%async_computation.3 | async-start | bytes 4456448 | tf_op jit(solution)/shard_map/all_gather | solution.py:106
Sparse Core Ops, SparseCore 0:
  9.8 105.2 all-gather.5
  117.5 101.7 all-gather.7
  221.1 49.3 all-gather.9
  272.1 47.8 all-gather.11
where the time goes:
time: 420 us; the launch traced here: 418 us
  waiting for transfers between devices  234 us (56%)
  matrix products  105 us (25%)
  other arithmetic  46 us (11%)
  local copies, waits for them, and re-layouts  18.5 us (4%)
  between operations  14.6 us (3%)
    all_gather x1, waiting for transfers between devices, shards(): lax.all_gather(prompt_values, 'sample', axis=0, tiled=True)  104 us
    all_gather x1, waiting for transfers between devices, shards(): lax.all_gather(prompt_keys, 'sample', axis=0, tiled=True)  91.1 us
    dot_general x16, matrix products, absorb(): jnp.einsum('agqk,kad->agqd', weights.astype(jnp.bfloat16), value_rows, pr...  64.2 us
    dot_general x16, matrix products, absorb(): jnp.einsum('agqd,kad->agqk', query_group, key_rows, preferred_element_typ...  40.5 us
    all_gather x1, waiting for transfers between devices, shards(): lax.all_gather(span_values[0], 'seq', axis=0, tiled=True)  38.5 us
    reduce_sum x16, other arithmetic, absorb(): new_sum = run_sum * fade_factor + jnp.sum(weights, axis=-1)  33.2 us
  transfers between devices with their start and end apart: 4, of which 3 were waited for; matrix products, arithmetic and copies ran while one was open for 18% of the time, Pallas kernels for 0%

commit v1 on v0

--- a/solution.py
+++ b/solution.py
@@ -94,7 +94,10 @@
         return lax.map(one_head, (grouped,) + tuple(carry_state) + (key_heads, value_split))
 
     shard_piece = (
-        lax.all_gather(prompt_keys, "sample", axis=0, tiled=True),
+        jnp.concatenate(
+            lax.all_to_all(jnp.stack([prompt_keys] * lax.axis_size("sample")), "sample", 0, 0),
+            axis=0,
+        ),
         lax.all_gather(prompt_values, "sample", axis=0, tiled=True),
     )
     after_prompt = by_head(initial, shard_piece[0], shard_piece[1], None)

time: 420 us -> 380 us (0.905)
  waiting for transfers between devices: 234 us -> 175 us
  starting transfers between devices: 0.13 us -> 11.8 us
  local copies, waits for them, and re-layouts: 18.5 us -> 25.9 us
    all_to_all x0 -> x1, waiting for transfers between devices: none -> 98.2 us  [shards(): lax.all_to_all(jnp.stack([prompt_keys] * lax.axis_size('sample')), 'sampl...]
    all_gather x1 -> x0, waiting for transfers between devices: 91.1 us -> none  [shards(): lax.all_gather(prompt_keys, 'sample', axis=0, tiled=True)]
    all_gather x1, waiting for transfers between devices: 104 us -> 37.2 us  [shards(): lax.all_gather(prompt_values, 'sample', axis=0, tiled=True)]
    all_to_all x0 -> x1, starting transfers between devices: none -> 11.8 us  [shards(): lax.all_to_all(jnp.stack([prompt_keys] * lax.axis_size('sample')), 'sampl...]
  transfers between devices with their start and end apart: 4 -> 4, of which waited for: 3 -> 3; matrix products, arithmetic and copies ran while one was open for 18% -> 22% of each run, Pallas kernels for 0% -> 0%
where the time goes in v1:
time: 380 us; the launch traced here: 378 us
  waiting for transfers between devices  175 us (46%)
  matrix products  105 us (28%)
  other arithmetic  46.1 us (12%)
  local copies, waits for them, and re-layouts  25.9 us (7%)
  between operations  14.6 us (4%)
  starting transfers between devices  11.8 us (3%)
    all_to_all x1, waiting for transfers between devices, shards(): lax.all_to_all(jnp.stack([prompt_keys] * lax.axis_size('sample')), 'sampl...  98.2 us
    dot_general x16, matrix products, absorb(): jnp.einsum('agqk,kad->agqd', weights.astype(jnp.bfloat16), value_rows, pr...  64.6 us
    dot_general x16, matrix products, absorb(): jnp.einsum('agqd,kad->agqk', query_group, key_rows, preferred_element_typ...  40.4 us
    all_gather x1, waiting for transfers between devices, shards(): lax.all_gather(span_values[0], 'seq', axis=0, tiled=True)  39.2 us
    all_gather x1, waiting for transfers between devices, shards(): lax.all_gather(prompt_values, 'sample', axis=0, tiled=True)  37.2 us
    reduce_sum x16, other arithmetic, absorb(): new_sum = run_sum * fade_factor + jnp.sum(weights, axis=-1)  33.2 us
    all_to_all x1, starting transfers between devices, shards(): lax.all_to_all(jnp.stack([prompt_keys] * lax.axis_size('sample')), 'sampl...  11.8 us
  transfers between devices with their start and end apart: 4, of which 3 were waited for; matrix products, arithmetic and copies ran while one was open for 22% of the time, Pallas kernels for 0%

profile of v1, /device:TPU:1, one launch (start us, length us, event | category | flops | bytes accessed | tf_op | source)
XLA Modules:
  0.0 378.5 jit_solution(8683975034971782056)
XLA Ops:
  6.5 1.8 copy.30
  11.2 3.4 stack.2
  14.7 11.8 %all-to-all-start = ((bf16[16,128,1024]{2,1,0:T(8,128)(2,1)}), bf16[16,128,1024]{2,1,0:T(8,128)(2,1)}, u32[]{:S(2)}, u32[]{:S(2)}) async-start(bf16[16,128,1024]{2,1,0:T(8,128)(2,1)} %stack.2), calls=%async_computation | async-start | bytes 8388608 | tf_op jit(solution)/shard_map/all_to_all | solution.py:98
  29.5 1.7 fusion.60
  31.1 4.9 %subtract_convert_fusion = (bf16[128,64,64]{2,0,1:T(8,128)(2,1)S(1)}, bf16[128,64,64]{2,0,1:T(8,128)(2,1)S(1)}) fusion(f32[128,64,64]{2,1,0:T(8,128)S(1)} %get-tuple-element.232, f32[128,64,64]{2,1,0:T(8,128)S(1)} %get-tuple-element.231, f32[128,64]{1,0:T(8,128)S(1)} %copy.29, f32[128,64]{1,0:T(8,128)S(1)} %copy.27), kind=kLoop, calls=%fused_computation.64 | loop fusion | flops 4194304 | bytes 6356992 | tf_op jit(solution)/shard_map/convert.7
  37.2 98.2 %all-to-all-done = bf16[16,128,1024]{2,1,0:T(8,128)(2,1)} async-done(((bf16[16,128,1024]{2,1,0:T(8,128)(2,1)}), bf16[16,128,1024]{2,1,0:T(8,128)(2,1)}, u32[]{:S(2)}, u32[]{:S(2)}) %all-to-all-start) | async-done | bytes 4194336 | tf_op jit(solution)/shard_map/all_to_all | solution.py:98
  135.4 3.3 copy.44
  138.7 2.6 copy.31
  141.3 37.2 %all-gather.5.cloned.1.call-done = bf16[2048,1024]{0,1:T(8,128)(2,1)} async-done(((bf16[128,1024]{0,1:T(8,128)(2,1)}), bf16[2048,1024]{0,1:T(8,128)(2,1)}) %all-gather.5.cloned.1.call-update) | async-done | bytes 4194320 | tf_op jit(solution)/shard_map/all_gather | solution.py:101
  178.5 62.3 %while.26 = (s32[]{:T(128)}, f32[8,1,8,128]{3,2,1,0:T(8,128)S(1)}, f32[8,1,8,128]{3,2,1,0:T(8,128)S(1)}, f32[8,1,8,128,128]{4,3,2,1,0:T(8,128)}, bf16[8,1,8,128,...) while((s32[]{:T(128)}, f32[8,1,8,128]{3,2,1,0:T(8,128)S(1)}, ...), condition=%wide.region_3.4_spmd, body=%wide.region_0.3_spmd.sunk | while | flops 1090655232 | bytes 27052128 | solution.py:94
  178.5 2.4 multiply_reduce_fusion.2
  180.9 1.6 fusion.75
  182.6 3.7 fusion.77
  186.3 2.4 multiply_reduce_fusion.2
  188.6 1.6 fusion.75
  190.3 3.7 fusion.77
  194.0 2.4 multiply_reduce_fusion.2
  196.4 1.6 fusion.75
  198.1 3.8 fusion.77
  201.9 2.4 multiply_reduce_fusion.2
  204.2 1.7 fusion.75
  205.9 3.7 fusion.77
  209.6 2.4 multiply_reduce_fusion.2
  212.0 1.6 fusion.75
  213.7 3.8 %fusion.77 = f32[8,1,8,128,128]{4,3,2,1,0:T(8,128)} fusion(f32[8,1,8,128,128]{4,3,2,1,0:T(8,128)} %get-tuple-element.405, s32[]{:T(128)S(6)} %copy.67, f32[8,128,2048]{2,1,0:T(8,128)S(1)} %get-tuple-element.341, f32[8,128]{1,0:T(8,128)S(1)} %get-tuple-element.343, bf16[8,2048,1,128]{1,3,0,2:T(8,128)(2,1)} %get-tuple-element.416, ...), kind=kOutput, calls=%fused_computation.7.clone.1 | convolution fusion | flops 543293440 | bytes 9446400 | tf_op jit(solution)/shard_map/while/body/eval_jaxpr/agqk,kad->agqd/dot_general | solution.py:47
  217.5 2.4 multiply_reduce_fusion.2
  221.5 3.7 fusion.77
  225.3 2.4 multiply_reduce_fusion.2
  227.6 1.6 fusion.75
  229.3 3.7 fusion.77
  233.0 2.4 multiply_reduce_fusion.2
  237.1 3.7 fusion.77
  240.8 39.2 %all-gather.9.cloned.1.call-done = bf16[1,2048,1024]{1,2,0:T(8,128)(2,1)} async-done(((bf16[1,128,1024]{1,2,0:T(8,128)(2,1)}), bf16[1,2048,1024]{1,2,0:T(8,128)(2,1)}) %all-gather.9.cloned.1.call-update) | async-done | bytes 4194320 | tf_op jit(solution)/shard_map/all_gather | solution.py:109
  280.2 81.6 %conditional.1 = ((f32[8,1,8,128]{3,2,1,0:T(8,128)S(1)}, f32[8,1,8,128,128]{4,3,2,1,0:T(8,128)})) conditional(s32[]{:T(128)} %convert_element_type.55, (f32[8,1,8,128]{3,2,1,0:T(8,128)S(1)}, f32[8,1,8,128,128]{4,3,2,1,0:T(8,128)}) %tuple.21, (bf16[2048,1024]{0,1:T(8,128)(2,1)}, bf16[2048,1024]{0,1:T(8,128)(2,1)}, s32[]{:T(128)}, ...), branch_computations={%region_4.5_spmd, %region_5.10_spmd} | conditional | flops 1101797504 | bytes 38149884 | solution.py:115
  280.5 76.6 %while.25 = (s32[]{:T(128)}, f32[8,1,8,128]{3,2,1,0:T(8,128)S(1)}, f32[8,1,8,128,128]{4,3,2,1,0:T(8,128)}, f32[8,1,8,128]{3,2,1,0:T(8,128)S(1)}, f32[8,1,8,128]{...) while((s32[]{:T(128)}, f32[8,1,8,128]{3,2,1,0:T(8,128)S(1)}, ...), condition=%wide.region_9.9_spmd, body=%wide.region_6.8_spmd.sunk | while | flops 1101271040 | bytes 28371068 | solution.py:94
  280.5 2.7 fusion.80
  283.2 2.5 fusion.82
  285.8 4.3 %fusion.84 = f32[8,1,8,128,128]{4,3,2,1,0:T(8,128)} fusion(f32[8,1,8,128,128]{4,3,2,1,0:T(8,128)} %get-tuple-element.374, s32[]{:T(128)S(6)} %copy.57, f32[8,128,2048]{2,1,0:T(8,128)S(1)} %get-tuple-element.357, f32[8,128]{1,0:T(8,128)S(1)} %get-tuple-element.359, pred[128,2048]{1,0:T(8,128)(4,1)S(1)} %get-tuple-element.388, ...), kind=kOutput, calls=%fused_computation.35.clone.1 | convolution fusion | flops 547618816 | bytes 10232832 | tf_op jit(solution)/shard_map/cond/branch_1_fun/while/body/eval_jaxpr/agqk,kad->agqd/dot_general | solution.py:47
  290.1 2.7 fusion.80
  292.8 2.5 fusion.82
  295.3 4.3 %fusion.84 = f32[8,1,8,128,128]{4,3,2,1,0:T(8,128)} fusion(f32[8,1,8,128,128]{4,3,2,1,0:T(8,128)} %get-tuple-element.374, s32[]{:T(128)S(6)} %copy.57, f32[8,128,2048]{2,1,0:T(8,128)S(1)} %get-tuple-element.357, f32[8,128]{1,0:T(8,128)S(1)} %get-tuple-element.359, pred[128,2048]{1,0:T(8,128)(4,1)S(1)} %get-tuple-element.388, ...), kind=kOutput, calls=%fused_computation.35.clone.1 | convolution fusion | flops 547618816 | bytes 10232832 | tf_op jit(solution)/shard_map/cond/branch_1_fun/while/body/eval_jaxpr/agqk,kad->agqd/dot_general | solution.py:47
  299.7 2.7 fusion.80
  302.4 2.5 fusion.82
  304.9 4.3 %fusion.84 = f32[8,1,8,128,128]{4,3,2,1,0:T(8,128)} fusion(f32[8,1,8,128,128]{4,3,2,1,0:T(8,128)} %get-tuple-element.374, s32[]{:T(128)S(6)} %copy.57, f32[8,128,2048]{2,1,0:T(8,128)S(1)} %get-tuple-element.357, f32[8,128]{1,0:T(8,128)S(1)} %get-tuple-element.359, pred[128,2048]{1,0:T(8,128)(4,1)S(1)} %get-tuple-element.388, ...), kind=kOutput, calls=%fused_computation.35.clone.1 | convolution fusion | flops 547618816 | bytes 10232832 | tf_op jit(solution)/shard_map/cond/branch_1_fun/while/body/eval_jaxpr/agqk,kad->agqd/dot_general | solution.py:47
  309.3 2.7 fusion.80
  312.0 2.5 fusion.82
  314.5 4.3 %fusion.84 = f32[8,1,8,128,128]{4,3,2,1,0:T(8,128)} fusion(f32[8,1,8,128,128]{4,3,2,1,0:T(8,128)} %get-tuple-element.374, s32[]{:T(128)S(6)} %copy.57, f32[8,128,2048]{2,1,0:T(8,128)S(1)} %get-tuple-element.357, f32[8,128]{1,0:T(8,128)S(1)} %get-tuple-element.359, pred[128,2048]{1,0:T(8,128)(4,1)S(1)} %get-tuple-element.388, ...), kind=kOutput, calls=%fused_computation.35.clone.1 | convolution fusion | flops 547618816 | bytes 10232832 | tf_op jit(solution)/shard_map/cond/branch_1_fun/while/body/eval_jaxpr/agqk,kad->agqd/dot_general | solution.py:47
  318.8 2.7 fusion.80
  321.5 2.5 fusion.82
  324.1 4.3 %fusion.84 = f32[8,1,8,128,128]{4,3,2,1,0:T(8,128)} fusion(f32[8,1,8,128,128]{4,3,2,1,0:T(8,128)} %get-tuple-element.374, s32[]{:T(128)S(6)} %copy.57, f32[8,128,2048]{2,1,0:T(8,128)S(1)} %get-tuple-element.357, f32[8,128]{1,0:T(8,128)S(1)} %get-tuple-element.359, pred[128,2048]{1,0:T(8,128)(4,1)S(1)} %get-tuple-element.388, ...), kind=kOutput, calls=%fused_computation.35.clone.1 | convolution fusion | flops 547618816 | bytes 10232832 | tf_op jit(solution)/shard_map/cond/branch_1_fun/while/body/eval_jaxpr/agqk,kad->agqd/dot_general | solution.py:47
  328.4 2.7 fusion.80
  331.1 2.5 fusion.82
  333.6 4.4 %fusion.84 = f32[8,1,8,128,128]{4,3,2,1,0:T(8,128)} fusion(f32[8,1,8,128,128]{4,3,2,1,0:T(8,128)} %get-tuple-element.374, s32[]{:T(128)S(6)} %copy.57, f32[8,128,2048]{2,1,0:T(8,128)S(1)} %get-tuple-element.357, f32[8,128]{1,0:T(8,128)S(1)} %get-tuple-element.359, pred[128,2048]{1,0:T(8,128)(4,1)S(1)} %get-tuple-element.388, ...), kind=kOutput, calls=%fused_computation.35.clone.1 | convolution fusion | flops 547618816 | bytes 10232832 | tf_op jit(solution)/shard_map/cond/branch_1_fun/while/body/eval_jaxpr/agqk,kad->agqd/dot_general | solution.py:47
  338.0 2.7 fusion.80
  340.7 2.5 fusion.82
  343.2 4.3 %fusion.84 = f32[8,1,8,128,128]{4,3,2,1,0:T(8,128)} fusion(f32[8,1,8,128,128]{4,3,2,1,0:T(8,128)} %get-tuple-element.374, s32[]{:T(128)S(6)} %copy.57, f32[8,128,2048]{2,1,0:T(8,128)S(1)} %get-tuple-element.357, f32[8,128]{1,0:T(8,128)S(1)} %get-tuple-element.359, pred[128,2048]{1,0:T(8,128)(4,1)S(1)} %get-tuple-element.388, ...), kind=kOutput, calls=%fused_computation.35.clone.1 | convolution fusion | flops 547618816 | bytes 10232832 | tf_op jit(solution)/shard_map/cond/branch_1_fun/while/body/eval_jaxpr/agqk,kad->agqd/dot_general | solution.py:47
  347.6 2.7 fusion.80
  350.3 2.5 fusion.82
  352.8 4.3 %fusion.84 = f32[8,1,8,128,128]{4,3,2,1,0:T(8,128)} fusion(f32[8,1,8,128,128]{4,3,2,1,0:T(8,128)} %get-tuple-element.374, s32[]{:T(128)S(6)} %copy.57, f32[8,128,2048]{2,1,0:T(8,128)S(1)} %get-tuple-element.357, f32[8,128]{1,0:T(8,128)S(1)} %get-tuple-element.359, pred[128,2048]{1,0:T(8,128)(4,1)S(1)} %get-tuple-element.388, ...), kind=kOutput, calls=%fused_computation.35.clone.1 | convolution fusion | flops 547618816 | bytes 10232832 | tf_op jit(solution)/shard_map/cond/branch_1_fun/while/body/eval_jaxpr/agqk,kad->agqd/dot_general | solution.py:47
  357.1 4.6 %copy.78 = f32[8,1,8,128,128]{4,3,2,1,0:T(8,128)} copy(f32[8,1,8,128,128]{4,3,2,1,0:T(8,128)} %get-tuple-element.421) | data formatting | bytes 8388608 | tf_op jit(solution)/shard_map/cond
  361.8 2.9 divide_bitcast_fusion
  364.7 2.7 copy.36
  367.3 2.8 reshape.316
  370.2 1.8 select_convert_fusion
  (71 shorter events, 9.8 us)
Async XLA Ops:
  6.5 172.0 %all-gather.5.cloned.1.call-start = ((), (), s32[]{:S(2)}) async-start(), calls=%async_computation.1 | async-start | bytes 4456448 | tf_op jit(solution)/shard_map/all_gather | solution.py:101
  8.4 232.5 %all-gather.7.cloned.1.call-start = ((), (), s32[]{:S(2)}) async-start(), calls=%async_computation.2 | async-start | bytes 4456448 | tf_op jit(solution)/shard_map/all_gather | solution.py:108
  14.7 11.8 %copy-start.1 = (bf16[1,128,1024]{2,1,0:T(8,128)(2,1)S(1)}, bf16[1,128,1024]{2,1,0:T(8,128)(2,1)}, u32[]{:S(2)}) copy-start(bf16[1,128,1024]{2,1,0:T(8,128)(2,1)} %param.15) | copy-start | bytes 786436
  14.7 13.6 %copy-start = (bf16[1,128,8192]{2,1,0:T(8,128)(2,1)S(1)}, bf16[1,128,8192]{2,1,0:T(8,128)(2,1)}, u32[]{:S(2)}) copy-start(bf16[1,128,8192]{2,1,0:T(8,128)(2,1)} %param.13) | copy-start | bytes 6291460
  14.7 120.7 %all-to-all-start = ((bf16[16,128,1024]{2,1,0:T(8,128)(2,1)}), bf16[16,128,1024]{2,1,0:T(8,128)(2,1)}, u32[]{:S(2)}, u32[]{:S(2)}) async-start(bf16[16,128,1024]{2,1,0:T(8,128)(2,1)} %stack.2), calls=%async_computation | async-start | bytes 8388608 | tf_op jit(solution)/shard_map/all_to_all | solution.py:98
  26.4 253.6 %all-gather.9.cloned.1.call-start = ((), (), s32[]{:S(2)}) async-start(), calls=%async_computation.3 | async-start | bytes 4456448 | tf_op jit(solution)/shard_map/all_gather | solution.py:109
Sparse Core Ops, SparseCore 0:
  9.8 168.6 all-gather.4
  180.2 50.2 all-gather.6
  232.3 47.7 all-gather.8
